TPU v7x, 256 devices: a whole 4x4x8 slice. The times are simulated.
256 devices in a mesh: det: 64 (over x, z, core), row: 4 (over y).
Axes of the slice: x: 4, y: 4, z: 8, core: 2. Of those that a mesh axis runs over, the one named last changes fastest.
Arguments:
- images: bfloat16 [384, 3, 384, 384], P('det', None, 'row'), may hold values from -6 to 6
- warp_rows: bfloat16 [384, 3, 384, 384], P('det', None, 'row'), may hold values from -0.3125 to 0.3125
- warp_cols: bfloat16 [384, 3, 384, 384], P('det'), may hold values from -0.3125 to 0.3125
- psf_coef: float32 [384, 3, 21], P('det'), may hold values from -1.25 to 1.25
- taps: float32 [21, 21], replicated, may hold values from -1.25 to 1.25
- dest_patch: int32 [3456, 1], replicated, may hold values from 0 to 63; in each aligned block of 54 rows (0 to 53, 54 to 107, ...) at most 2 rows name the same one
- dest_block: int32 [3456], replicated, may hold values from 0 to 2
- weight_index: int32 [384, 3], replicated, may hold values from 0 to 7
- weight_table: float32 [8], replicated, may hold values from 0.25 to 4
- patch_home: int32 [64], replicated, may hold values from 0 to 63, each once
Outputs:
- difference: bfloat16 [384, 3, 384, 384], P('det', None, 'row')
- coadd: bfloat16 [64, 384, 384], P('det', 'row')
Inputs may be any that keep to these rules, and one draw needn't show every extreme that they name: `dest_patch`: within the 54 rows of one device (an aligned block of rows), no patch is named more than 2 times. `patch_home`: each position once.
All inputs are finite; a program needn't handle non-finite values.
Results may differ from a plain program's by a relative error of at most 0.0082.
Values may be sent and summed in bfloat16 or wider, within the bound.
A program may use at most 128 MiB of HBM per device.

v0:
```python
import jax
import jax.numpy as jnp
from jax import lax
from jax.sharding import PartitionSpec as P

TILE = 128


def extended(value, sides, width):
    for axis, dim in sides:
        size, length = (lax.axis_size(axis), value.shape[dim])
        up = [(i, (i + 1) % size) for i in range(size - 1)]
        down = [(j, i) for i, j in up]
        last = lax.slice_in_dim(value, length - width, length, axis=dim)
        first = lax.slice_in_dim(value, 0, width, axis=dim)
        before = lax.ppermute(last, axis, up)
        after = lax.ppermute(first, axis, down)
        value = jnp.concatenate([before, value, after], axis=dim)
    return value


def toeplitz_table(values, out_len, in_len):
    span_len = values.shape[1]
    offsets = jnp.arange(in_len)[None, :] - jnp.arange(out_len)[:, None]
    picks = (offsets[:, :, None] == jnp.arange(span_len)[None, None, :]).astype(jnp.float32)
    return jnp.einsum("oij,kj->koi", picks, values.astype(jnp.float32)).astype(jnp.bfloat16)


def per_device(
    images,
    warp_rows,
    warp_cols,
    psf_coef,
    taps,
    dest_patch,
    dest_block,
    weight_index,
    weight_table,
    patch_home,
):
    det_count, visit_count, band_rows, side_cols = images.shape
    kernel_count, tap_count = taps.shape
    reach = (tap_count - 1) // 2
    tile_cols = TILE
    tile_count = side_cols // tile_cols
    det_devices = lax.axis_size("det")
    my_index = lax.axis_index("det")
    image_count = det_count * visit_count
    piece_count = image_count * tile_count
    capacity = max(2, 2 * ((piece_count + det_devices - 1) // det_devices))
    slot_count = det_devices * capacity
    padded_rows = band_rows + 2 * reach
    col_warped = jnp.einsum(
        "dvbs,dvst->dvbt", images, warp_cols, preferred_element_type=jnp.float32
    ).astype(jnp.bfloat16)
    warped = jnp.einsum(
        "dvbr,dvrs->dvbs",
        warp_rows,
        lax.all_gather(col_warped, "row", axis=2, tiled=True),
        preferred_element_type=jnp.float32,
    ).astype(jnp.bfloat16)
    padded = extended(warped, (("row", 2),), reach)
    taps_half = taps.astype(jnp.bfloat16)
    col_table = toeplitz_table(taps_half, tile_cols, tile_cols + 2 * reach)
    tiles_in = padded.reshape(image_count, padded_rows, side_cols)
    coef_rows = psf_coef.reshape(image_count, kernel_count)

    def match_image(inputs):
        tile_image, coef_row = inputs
        widened = jnp.pad(tile_image, ((0, 0), (reach, reach)))
        windows = jnp.stack(
            [
                widened[
                    :, column_tile * tile_cols : column_tile * tile_cols + tile_cols + 2 * reach
                ]
                for column_tile in range(tile_count)
            ],
            axis=1,
        )
        conv_cols = jnp.einsum(
            "rtw,kcw->krtc", windows, col_table, preferred_element_type=jnp.float32
        ).astype(jnp.bfloat16)
        conv_cols = conv_cols.reshape(kernel_count, padded_rows, side_cols)
        scaled = (coef_row[:, None] * taps).astype(jnp.bfloat16)
        row_table = toeplitz_table(scaled, band_rows, padded_rows)
        return jnp.einsum("kbr,krs->bs", row_table, conv_cols, preferred_element_type=jnp.float32)

    matched = lax.map(match_image, (tiles_in, coef_rows))
    level_count = weight_table.shape[0]
    level_onehot = (weight_index[:, :, None] == jnp.arange(level_count)[None, None, :]).astype(
        jnp.float32
    )
    weight_all = jnp.sum(level_onehot * weight_table[None, None, :], axis=2)
    weight_mine = lax.dynamic_slice_in_dim(weight_all, my_index * det_count, det_count, 0).reshape(
        image_count
    )
    weighted = (
        (weight_mine[:, None, None] * matched)
        .astype(jnp.bfloat16)
        .reshape(image_count, band_rows, tile_count, tile_cols)
    )
    patch_count = patch_home.shape[0]
    patch_ids = dest_patch[:, 0]
    owner_all = jnp.sum(
        jnp.where(patch_ids[:, None] == jnp.arange(patch_count)[None, :], patch_home[None, :], 0),
        axis=1,
    )
    owner_grid = owner_all.reshape(det_devices, piece_count)
    earlier = jnp.arange(piece_count)[None, :] < jnp.arange(piece_count)[:, None]
    rank_grid = jnp.sum(
        ((owner_grid[:, :, None] == owner_grid[:, None, :]) & earlier[None]).astype(jnp.int32),
        axis=2,
    )
    slot_grid = owner_grid * capacity + rank_grid
    slot_mine = lax.dynamic_slice_in_dim(slot_grid, my_index, 1, 0)[0]
    send_pick = (
        (jnp.arange(slot_count)[:, None] == slot_mine[None, :])
        .astype(jnp.bfloat16)
        .reshape(slot_count, image_count, tile_count)
    )
    weight_pieces = jnp.repeat(weight_all.reshape(-1), tile_count)
    to_mine = owner_all == my_index
    block_onehot = (dest_block[:, None] == jnp.arange(tile_count)[None, :]).astype(jnp.float32)
    denominator = jnp.sum(
        jnp.where(to_mine[:, None], block_onehot * weight_pieces[:, None], 0.0), axis=0
    )
    source_slot = jnp.arange(
        det_devices * piece_count
    ) // piece_count * capacity + rank_grid.reshape(-1)
    slot_onehot = (
        (source_slot[:, None] == jnp.arange(slot_count)[None, :]) & to_mine[:, None]
    ).astype(jnp.float32)
    gather_matrix = jnp.einsum("iq,is->qs", block_onehot, slot_onehot).astype(jnp.bfloat16)
    outgoing = jnp.einsum(
        "spq,pbqc->sbc", send_pick, weighted, preferred_element_type=jnp.float32
    ).astype(jnp.bfloat16)
    received = lax.all_to_all(outgoing, "det", split_axis=0, concat_axis=0, tiled=True)
    numerator = jnp.einsum(
        "qs,sbc->bqc", gather_matrix, received, preferred_element_type=jnp.float32
    )
    template = (numerator / jnp.maximum(denominator, 1.0)[None, :, None]).astype(jnp.bfloat16)
    coadd_band = template.reshape(1, band_rows, side_cols)
    returned = jnp.einsum(
        "qs,bqc->sbc", gather_matrix, template, preferred_element_type=jnp.float32
    ).astype(jnp.bfloat16)
    arrived = lax.all_to_all(returned, "det", split_axis=0, concat_axis=0, tiled=True)
    local_template = jnp.einsum(
        "spq,sbc->pbqc", send_pick, arrived, preferred_element_type=jnp.float32
    )
    difference = (
        matched.reshape(image_count, band_rows, tile_count, tile_cols) - local_template
    ).astype(jnp.bfloat16)
    difference = difference.reshape(det_count, visit_count, band_rows, side_cols)
    return (difference, coadd_band)


def solution(mesh):
    placed = (
        P("det", None, "row", None),
        P("det", None, "row", None),
        P("det", None, None, None),
        P("det", None, None),
        P(),
        P(),
        P(),
        P(),
        P(),
        P(),
    )
    return jax.shard_map(
        per_device,
        mesh=mesh,
        in_specs=placed,
        out_specs=(P("det", None, "row", None), P("det", "row", None)),
        check_vma=False,
    )
```

profile of v0, /device:TPU:1, one launch (start us, length us, event | category | flops | bytes accessed | tf_op | source)
XLA Modules:
  0.0 490.7 jit_solution(14183806398760456192)
XLA Ops:
  8.5 4.7 convolution_convert_fusion.3
  15.2 62.1 %all-gather.2.cloned.1.call-done = bf16[6,3,384,384]{3,2,1,0:T(8,128)(2,1)} async-done(((bf16[6,3,96,384]{3,2,1,0:T(8,128)(2,1)}), bf16[6,3,384,384]{3,2,1,0:T(8,128)(2,1)}) %all-gather.2.cloned.1.call-update) | async-done | bytes 5308432 | tf_op jit(solution)/shard_map/all_gather | solution.py:59
  77.3 3.6 fusion.26
  81.0 2.7 collective-permute-start
  87.8 3.8 collective-permute-done.1
  93.4 198.1 %while.12 = (s32[]{:T(128)}, f32[18,96,384]{2,1,0:T(8,128)}, f32[18,21]{1,0:T(8,128)S(1)}, f32[21,21]{1,0:T(8,128)S(1)}, bf16[18,116,384]{2,1,0:T(8,128)(2,1)}, /*index=5*/bf16[21,128,148]{1,2,0:T(8,128)(2,1)}, s32[]{:T(128)}) while((s32[]{:T(128)}, f32[18,96,384]{2,1,0:T(8,128)}, f32[18,21]{1,0:T(8,128)S(1)}, f32[21,21]{1,0:T(8,128)S(1)}, ...), condition=%wide.region_1.2_spmd, body=%wide.region_0.1_spmd.sunk | while | flops 468033056 | bytes 10274817 | solution.py:88
  95.7 3.2 convert_bitcast_fusion.2
  98.9 3.0 copy.109
  101.9 2.5 fusion.84
  106.7 3.2 convert_bitcast_fusion.2
  109.9 3.0 copy.109
  117.7 3.2 convert_bitcast_fusion.2
  120.9 3.0 copy.109
  123.9 2.5 fusion.84
  128.7 3.2 convert_bitcast_fusion.2
  131.9 3.0 copy.109
  134.9 2.5 fusion.84
  139.7 3.2 convert_bitcast_fusion.2
  142.9 3.0 copy.109
  150.7 3.2 convert_bitcast_fusion.2
  153.9 3.0 copy.109
  161.7 3.2 convert_bitcast_fusion.2
  164.9 3.0 copy.109
  167.9 2.5 fusion.84
  172.7 3.2 convert_bitcast_fusion.2
  175.9 3.0 copy.109
  183.7 3.2 convert_bitcast_fusion.2
  186.9 3.0 copy.109
  189.9 2.5 fusion.84
  194.7 3.2 convert_bitcast_fusion.2
  197.9 3.0 copy.109
  200.9 2.5 fusion.84
  205.7 3.2 convert_bitcast_fusion.2
  208.9 3.0 copy.109
  216.7 3.2 convert_bitcast_fusion.2
  219.9 3.0 copy.109
  222.9 2.5 fusion.84
  227.7 3.2 convert_bitcast_fusion.2
  230.9 3.0 copy.109
  238.7 3.2 convert_bitcast_fusion.2
  241.9 3.0 copy.109
  244.9 2.5 fusion.84
  249.7 3.2 convert_bitcast_fusion.2
  252.9 3.0 copy.109
  255.9 2.5 fusion.84
  260.7 3.2 convert_bitcast_fusion.2
  263.9 3.0 copy.109
  267.0 2.5 fusion.84
  271.7 3.2 convert_bitcast_fusion.2
  274.9 3.0 copy.109
  278.0 2.5 fusion.84
  282.7 3.2 convert_bitcast_fusion.2
  285.9 3.0 copy.109
  289.0 2.5 fusion.84
  291.5 3.1 multiply_convert_fusion.1
  294.5 3.6 reshape.134
  300.1 3.7 copy.71
  303.8 12.1 %all-to-all-start = ((bf16[128,96,128]{2,1,0:T(8,128)(2,1)}), bf16[128,96,128]{2,1,0:T(8,128)(2,1)}, u32[]{:S(2)}, u32[]{:S(2)}) async-start(bf16[128,96,128]{2,1,0:T(8,128)(2,1)} %copy.71), calls=%async_computation | async-start | bytes 6291456 | tf_op jit(solution)/shard_map/all_to_all | solution.py:137
  318.4 71.0 %all-to-all-done = bf16[128,96,128]{2,1,0:T(8,128)(2,1)} async-done(((bf16[128,96,128]{2,1,0:T(8,128)(2,1)}), bf16[128,96,128]{2,1,0:T(8,128)(2,1)}, u32[]{:S(2)}, u32[]{:S(2)}) %all-to-all-start) | async-done | bytes 3145760 | tf_op jit(solution)/shard_map/all_to_all | solution.py:137
  389.4 2.8 fusion.34
  393.3 3.7 copy.74
  397.0 6.2 %all-to-all-start.1 = ((bf16[128,96,128]{2,1,0:T(8,128)(2,1)}), bf16[128,96,128]{2,1,0:T(8,128)(2,1)}, u32[]{:S(2)}, u32[]{:S(2)}) async-start(bf16[128,96,128]{2,1,0:T(8,128)(2,1)} %copy.74), calls=%async_computation.1 | async-start | bytes 6291456 | tf_op jit(solution)/shard_map/all_to_all | solution.py:146
  403.9 72.7 %all-to-all-done.1 = bf16[128,96,128]{2,1,0:T(8,128)(2,1)} async-done(((bf16[128,96,128]{2,1,0:T(8,128)(2,1)}), bf16[128,96,128]{2,1,0:T(8,128)(2,1)}, u32[]{:S(2)}, u32[]{:S(2)}) %all-to-all-start.1) | async-done | bytes 3145760 | tf_op jit(solution)/shard_map/all_to_all | solution.py:146
  476.7 3.3 fusion.15
  (175 shorter events, 75.0 us)
Async XLA Ops:
  7.2 1.3 copy-start
  7.2 6.1 %copy-start.9 = (f32[8]{0:T(128)S(1)}, f32[8]{0:T(128)}, u32[]{:S(2)}) copy-start(f32[8]{0:T(128)} %param.20) | copy-start | bytes 100
  7.2 6.1 %copy-start.7 = (s32[384,3]{0,1:T(4,128)S(1)}, s32[384,3]{0,1:T(4,128)}, u32[]{:S(2)}) copy-start(s32[384,3]{0,1:T(4,128)} %param.19) | copy-start | bytes 13828
  7.2 6.4 %copy-start.6 = (f32[6,3,21]{2,1,0:T(4,128)S(1)}, f32[6,3,21]{2,1,0:T(4,128)}, u32[]{:S(2)}) copy-start(f32[6,3,21]{2,1,0:T(4,128)} %param.15) | copy-start | bytes 4540
  7.2 6.4 %copy-start.5 = (s32[3456,1]{0,1:T(1,128)S(1)}, s32[3456,1]{0,1:T(1,128)}, u32[]{:S(2)}) copy-start(s32[3456,1]{0,1:T(1,128)} %param.17) | copy-start | bytes 41476
  7.2 6.5 %copy-start.8 = (s32[64]{0:T(128)S(1)}, s32[64]{0:T(128)}, u32[]{:S(2)}) copy-start(s32[64]{0:T(128)} %param.21) | copy-start | bytes 772
  7.2 70.1 %all-gather.2.cloned.1.call-start = ((), (), s32[]{:S(2)}) async-start(), calls=%async_computation.2 | async-start | bytes 6635520 | tf_op jit(solution)/shard_map/all_gather | solution.py:59
  13.2 64.1 %copy-start.2 = (bf16[6,3,96,384]{3,2,1,0:T(8,128)(2,1)S(1)}, bf16[6,3,96,384]{3,2,1,0:T(8,128)(2,1)}, u32[]{:S(2)}) copy-start(bf16[6,3,96,384]{3,2,1,0:T(8,128)(2,1)} %param.13) | copy-start | bytes 3981316
  15.2 69.8 %copy-start.3 = (f32[21,21]{1,0:T(8,128)S(1)}, f32[21,21]{1,0:T(8,128)}, u32[]{:S(2)}) copy-start(f32[21,21]{1,0:T(8,128)} %param.16) | copy-start | bytes 5296
  81.0 6.7 %collective-permute-start = (bf16[6,3,10,384]{3,2,1,0:T(8,128)(2,1)S(1)}, bf16[6,3,10,384]{3,2,1,0:T(8,128)(2,1)S(1)}, u32[]{:S(2)}, u32[]{:S(2)}) collective-permute-start(bf16[6,3,10,384]{3,2,1,0:T(8,128)(2,1)S(1)} %get-tuple-element.125), channel_id=1, source_target_pairs={{0,1},{1,2},{2,3},{4,5},{5,6},{6,7},{8,9},{9,10},{10,11},{12,13},{... | collective-permute-start | bytes 414728 | tf_op jit(solution)/shard_map/ppermute | solution.py:16
  83.7 7.9 %collective-permute-start.1 = (bf16[6,3,10,384]{3,2,1,0:T(8,128)(2,1)S(1)}, bf16[6,3,10,384]{3,2,1,0:T(8,128)(2,1)S(1)}, u32[]{:S(2)}, u32[]{:S(2)}) collective-permute-start(bf16[6,3,10,384]{3,2,1,0:T(8,128)(2,1)S(1)} %get-tuple-element.126), channel_id=1, source_target_pairs={{1,0},{2,1},{3,2},{5,4},{6,5},{7,6},{9,8},{10,9},{11,10},{13,12},{... | collective-permute-start | bytes 414728 | tf_op jit(solution)/shard_map/ppermute | solution.py:17
  303.8 13.3 %copy-start.4 = (s32[3456]{0:T(1024)S(1)}, s32[3456]{0:T(1024)}, u32[]{:S(2)}) copy-start(s32[3456]{0:T(1024)} %param.18) | copy-start | bytes 41476
  303.8 85.6 %all-to-all-start = ((bf16[128,96,128]{2,1,0:T(8,128)(2,1)}), bf16[128,96,128]{2,1,0:T(8,128)(2,1)}, u32[]{:S(2)}, u32[]{:S(2)}) async-start(bf16[128,96,128]{2,1,0:T(8,128)(2,1)} %copy.71), calls=%async_computation | async-start | bytes 6291456 | tf_op jit(solution)/shard_map/all_to_all | solution.py:137
  397.0 79.7 %all-to-all-start.1 = ((bf16[128,96,128]{2,1,0:T(8,128)(2,1)}), bf16[128,96,128]{2,1,0:T(8,128)(2,1)}, u32[]{:S(2)}, u32[]{:S(2)}) async-start(bf16[128,96,128]{2,1,0:T(8,128)(2,1)} %copy.74), calls=%async_computation.1 | async-start | bytes 6291456 | tf_op jit(solution)/shard_map/all_to_all | solution.py:146
  476.7 3.3 copy-start.1
Sparse Core Ops, SparseCore 0:
  13.4 63.8 all-gather.1
where the time goes:
time: 495 us; the launch traced here: 491 us
  waiting for transfers between devices  211 us (43%)
  matrix products  143 us (29%)
  local copies, waits for them, and re-layouts  92.9 us (19%)
  starting transfers between devices  22.4 us (5%)
  between operations  14.4 us (3%)
  other arithmetic  7.01 us (1%)
    all_to_all x1, waiting for transfers between devices, per_device(): lax.all_to_all(returned, 'det', split_axis=0, concat_axis=0, tiled=True)  72.7 us
    all_to_all x1, waiting for transfers between devices, per_device(): lax.all_to_all(outgoing, 'det', split_axis=0, concat_axis=0, tiled=True)  71 us
    all_gather x1, waiting for transfers between devices, per_device(): lax.all_gather(col_warped, 'row', axis=2, tiled=True)  62.1 us
    dot_general x18, matrix products, match_image(): jnp.einsum('rtw,kcw->krtc', windows, col_table, preferred_element_type=jn...  57.4 us
    convert_element_type x18, local copies, waits for them, and re-layouts, match_image(): conv_cols = jnp.einsum('rtw,kcw->krtc', windows, col_table, preferred_ele...  54.3 us
    dot_general x18, matrix products, match_image(): jnp.einsum('kbr,krs->bs', row_table, conv_cols, preferred_element_type=jn...  44.7 us
    dot_general x19, matrix products, toeplitz_table(): jnp.einsum('oij,kj->koi', picks, values.astype(jnp.float32))  22.1 us
    dynamic_slice x36, local copies, waits for them, and re-layouts, per_device(): matched = lax.map(match_image, (tiles_in, coef_rows))  18.7 us
  transfers between devices with their start and end apart: 5, of which 5 were waited for; matrix products, arithmetic and copies ran while one was open for 1% of the time, Pallas kernels for 0%

commit v1 on v0

--- a/solution.py
+++ b/solution.py
@@ -4,6 +4,24 @@
 from jax.sharding import PartitionSpec as P
 
 TILE = 128
+
+
+def gather_around(value, axis, dim):
+    ways, here, step = (lax.axis_size(axis), lax.axis_index(axis), value.shape[dim])
+    lengths = [n * ways if d == dim else n for d, n in enumerate(value.shape)]
+    full = lax.dynamic_update_slice_in_dim(
+        jnp.zeros(lengths, value.dtype), value, here * step, axis=dim
+    )
+    going_up = going_down = value
+    for far in range(1, ways // 2 + 1):
+        going_up = lax.ppermute(going_up, axis, [(d, (d + 1) % ways) for d in range(ways)])
+        full = lax.dynamic_update_slice_in_dim(full, going_up, (here - far) % ways * step, axis=dim)
+        if 2 * far < ways:
+            going_down = lax.ppermute(going_down, axis, [(d, (d - 1) % ways) for d in range(ways)])
+            full = lax.dynamic_update_slice_in_dim(
+                full, going_down, (here + far) % ways * step, axis=dim
+            )
+    return full
 
 
 def extended(value, sides, width):
@@ -56,7 +74,7 @@
     warped = jnp.einsum(
         "dvbr,dvrs->dvbs",
         warp_rows,
-        lax.all_gather(col_warped, "row", axis=2, tiled=True),
+        gather_around(col_warped, "row", 2),
         preferred_element_type=jnp.float32,
     ).astype(jnp.bfloat16)
     padded = extended(warped, (("row", 2),), reach)

time: 495 us -> 451 us (0.911)
  matrix products: 143 us -> 106 us
  waiting for transfers between devices: 211 us -> 196 us
  between operations: 14.4 us -> 0.91 us
  local copies, waits for them, and re-layouts: 92.9 us -> 104 us
  starting transfers between devices: 22.4 us -> 31.9 us
    all_gather x1 -> x0, waiting for transfers between devices: 62.1 us -> none  [per_device(): lax.all_gather(col_warped, 'row', axis=2, tiled=True)]
    ppermute x0 -> x3, waiting for transfers between devices: none -> 47.6 us  [the longest x2 47.6 us: gather_around(): lax.ppermute(going_up, axis, [(d, (d + 1) % ways) for d in range(ways)])]
    dot_general x18, matrix products: 44.7 us -> 25.3 us  [match_image(): jnp.einsum('kbr,krs->bs', row_table, conv_cols, preferred_element_type=jn...]
    dot_general x19, matrix products: 22.1 us -> 7.16 us  [toeplitz_table(): jnp.einsum('oij,kj->koi', picks, values.astype(jnp.float32))]
    dynamic_update_slice x0 -> x3, local copies, waits for them, and re-layouts: none -> 7.75 us  [the longest x2 5.11 us: gather_around(): lax.dynamic_update_slice_in_dim(full, going_up, (here - far) % ways * ste...]
    ppermute x0 -> x3, starting transfers between devices: none -> 5.22 us  [the longest x2 3.66 us: gather_around(): lax.ppermute(going_up, axis, [(d, (d + 1) % ways) for d in range(ways)])]
  transfers between devices with their start and end apart: 5 -> 7, of which waited for: 5 -> 6; matrix products, arithmetic and copies ran while one was open for 1% -> 3% of each run, Pallas kernels for 0% -> 0%
where the time goes in v1:
time: 451 us; the launch traced here: 448 us
  waiting for transfers between devices  196 us (43%)
  matrix products  106 us (24%)
  local copies, waits for them, and re-layouts  104 us (23%)
  starting transfers between devices  31.9 us (7%)
  other arithmetic  7.94 us (2%)
    all_to_all x1, waiting for transfers between devices, per_device(): lax.all_to_all(returned, 'det', split_axis=0, concat_axis=0, tiled=True)  72.7 us
    all_to_all x1, waiting for transfers between devices, per_device(): lax.all_to_all(outgoing, 'det', split_axis=0, concat_axis=0, tiled=True)  71 us
    dot_general x18, matrix products, match_image(): jnp.einsum('rtw,kcw->krtc', windows, col_table, preferred_element_type=jn...  57.2 us
    convert_element_type x18, local copies, waits for them, and re-layouts, match_image(): conv_cols = jnp.einsum('rtw,kcw->krtc', windows, col_table, preferred_ele...  54.3 us
    ppermute x2, waiting for transfers between devices, gather_around(): lax.ppermute(going_up, axis, [(d, (d + 1) % ways) for d in range(ways)])  47.6 us
    dot_general x18, matrix products, match_image(): jnp.einsum('kbr,krs->bs', row_table, conv_cols, preferred_element_type=jn...  25.3 us
    dynamic_slice x36, local copies, waits for them, and re-layouts, per_device(): matched = lax.map(match_image, (tiles_in, coef_rows))  18.5 us
    all_to_all x1, starting transfers between devices, per_device(): lax.all_to_all(outgoing, 'det', split_axis=0, concat_axis=0, tiled=True)  16.2 us
  transfers between devices with their start and end apart: 7, of which 6 were waited for; matrix products, arithmetic and copies ran while one was open for 3% of the time, Pallas kernels for 0%

profile of v1, /device:TPU:1, one launch (start us, length us, event | category | flops | bytes accessed | tf_op | source)
XLA Modules:
  0.0 447.6 jit_solution(17785696101246625873)
XLA Ops:
  0.7 3.4 broadcast_in_dim.37
  5.5 2.4 constant_dynamic-update-slice_fusion.3
  7.9 2.2 collective-permute-start
  10.0 1.6 collective-permute-start.1
  11.6 26.8 %collective-permute-done = bf16[6,3,96,384]{3,2,1,0:T(8,128)(2,1)} collective-permute-done((bf16[6,3,96,384]{3,2,1,0:T(8,128)(2,1)S(1)}, bf16[6,3,96,384]{3,2,1,0:T(8,128)(2,1)}, u32[]{:S(2)}, u32[]{:S(2)}) %collective-permute-start) | collective-permute-done | bytes 1327136 | tf_op jit(solution)/shard_map/ppermute | solution.py:17
  38.4 1.5 collective-permute-start.2
  42.3 2.6 constant_dynamic-update-slice_fusion.2
  44.9 2.6 constant_dynamic-update-slice_fusion.1
  47.5 20.7 %collective-permute-done.2 = bf16[6,3,96,384]{3,2,1,0:T(8,128)(2,1)} collective-permute-done((bf16[6,3,96,384]{3,2,1,0:T(8,128)(2,1)}, bf16[6,3,96,384]{3,2,1,0:T(8,128)(2,1)}, u32[]{:S(2)}, u32[]{:S(2)}) %collective-permute-start.2) | collective-permute-done | bytes 1327136 | tf_op jit(solution)/shard_map/ppermute | solution.py:17
  68.3 2.5 constant_dynamic-update-slice_fusion
  70.8 3.7 fusion.26
  74.6 2.7 collective-permute-start.3
  77.4 1.5 collective-permute-start.4
  80.2 4.2 collective-permute-done.4
  84.4 2.7 pad_maximum_fusion
  87.1 164.0 %while.12 = (s32[]{:T(128)}, f32[18,96,384]{2,1,0:T(8,128)}, f32[18,21]{1,0:T(8,128)S(1)}, f32[21,21]{1,0:T(8,128)S(1)}, bf16[18,116,384]{2,1,0:T(8,128)(2,1)}, /*index=5*/bf16[21,128,148]{1,2,0:T(8,128)(2,1)}, s32[]{:T(128)}) while((s32[]{:T(128)}, f32[18,96,384]{2,1,0:T(8,128)}, f32[18,21]{1,0:T(8,128)S(1)}, f32[21,21]{1,0:T(8,128)S(1)}, ...), condition=%wide.region_1.2_spmd, body=%wide.region_0.1_spmd.sunk | while | flops 468033056 | bytes 10153205 | solution.py:106
  88.2 3.2 convert_bitcast_fusion.2
  91.4 3.0 copy.109
  97.3 3.2 convert_bitcast_fusion.2
  100.5 3.0 copy.109
  106.5 3.2 convert_bitcast_fusion.2
  109.6 3.0 copy.109
  115.6 3.2 convert_bitcast_fusion.2
  118.7 3.0 copy.109
  124.7 3.2 convert_bitcast_fusion.2
  127.8 3.0 copy.109
  133.8 3.2 convert_bitcast_fusion.2
  137.0 3.0 copy.109
  142.9 3.2 convert_bitcast_fusion.2
  146.1 3.0 copy.109
  152.0 3.2 convert_bitcast_fusion.2
  155.2 3.0 copy.109
  161.1 3.2 convert_bitcast_fusion.2
  164.3 3.0 copy.109
  170.2 3.2 convert_bitcast_fusion.2
  173.4 3.0 copy.109
  179.3 3.2 convert_bitcast_fusion.2
  182.5 3.0 copy.109
  188.5 3.2 convert_bitcast_fusion.2
  191.6 3.0 copy.109
  197.6 3.2 convert_bitcast_fusion.2
  200.7 3.0 copy.109
  206.7 3.2 convert_bitcast_fusion.2
  209.9 3.0 copy.109
  215.8 3.2 convert_bitcast_fusion.2
  219.0 3.0 copy.109
  224.9 3.2 convert_bitcast_fusion.2
  228.1 3.0 copy.109
  234.0 3.2 convert_bitcast_fusion.2
  237.2 3.0 copy.109
  243.1 3.2 convert_bitcast_fusion.2
  246.3 3.0 copy.109
  251.1 3.1 multiply_convert_fusion.1
  254.2 3.6 reshape.134
  257.8 1.9 bitcast_convert_fusion
  259.8 3.7 copy.71
  263.5 16.2 %all-to-all-start = ((bf16[128,96,128]{2,1,0:T(8,128)(2,1)}), bf16[128,96,128]{2,1,0:T(8,128)(2,1)}, u32[]{:S(2)}, u32[]{:S(2)}) async-start(bf16[128,96,128]{2,1,0:T(8,128)(2,1)} %copy.71), calls=%async_computation | async-start | bytes 6291456 | tf_op jit(solution)/shard_map/all_to_all | solution.py:155
  282.1 71.0 %all-to-all-done = bf16[128,96,128]{2,1,0:T(8,128)(2,1)} async-done(((bf16[128,96,128]{2,1,0:T(8,128)(2,1)}), bf16[128,96,128]{2,1,0:T(8,128)(2,1)}, u32[]{:S(2)}, u32[]{:S(2)}) %all-to-all-start) | async-done | bytes 3145760 | tf_op jit(solution)/shard_map/all_to_all | solution.py:155
  353.1 2.8 fusion.34
  357.0 3.7 copy.74
  360.8 6.3 %all-to-all-start.1 = ((bf16[128,96,128]{2,1,0:T(8,128)(2,1)}), bf16[128,96,128]{2,1,0:T(8,128)(2,1)}, u32[]{:S(2)}, u32[]{:S(2)}) async-start(bf16[128,96,128]{2,1,0:T(8,128)(2,1)} %copy.74), calls=%async_computation.1 | async-start | bytes 6291456 | tf_op jit(solution)/shard_map/all_to_all | solution.py:164
  367.7 72.7 %all-to-all-done.1 = bf16[128,96,128]{2,1,0:T(8,128)(2,1)} async-done(((bf16[128,96,128]{2,1,0:T(8,128)(2,1)}), bf16[128,96,128]{2,1,0:T(8,128)(2,1)}, u32[]{:S(2)}, u32[]{:S(2)}) %all-to-all-start.1) | async-done | bytes 3145760 | tf_op jit(solution)/shard_map/all_to_all | solution.py:164
  440.5 3.3 fusion.15
  445.3 2.3 reshape.136
  (184 shorter events, 62.5 us)
Async XLA Ops:
  0.6 3.4 copy-start
  0.6 4.8 %copy-start.2 = (bf16[6,3,384,384]{3,2,1,0:T(8,128)(2,1)S(1)}, bf16[6,3,384,384]{3,2,1,0:T(8,128)(2,1)}, u32[]{:S(2)}) copy-start(bf16[6,3,384,384]{3,2,1,0:T(8,128)(2,1)} %param.14) | copy-start | bytes 15925252
  5.5 34.4 %copy-start.4 = (f32[21,21]{1,0:T(8,128)S(1)}, f32[21,21]{1,0:T(8,128)}, u32[]{:S(2)}) copy-start(f32[21,21]{1,0:T(8,128)} %param.16) | copy-start | bytes 5296
  7.8 33.6 %copy-start.7 = (f32[6,3,21]{2,1,0:T(4,128)S(1)}, f32[6,3,21]{2,1,0:T(4,128)}, u32[]{:S(2)}) copy-start(f32[6,3,21]{2,1,0:T(4,128)} %param.15) | copy-start | bytes 4540
  7.8 33.6 %copy-start.8 = (s32[384,3]{0,1:T(4,128)S(1)}, s32[384,3]{0,1:T(4,128)}, u32[]{:S(2)}) copy-start(s32[384,3]{0,1:T(4,128)} %param.19) | copy-start | bytes 13828
  7.8 33.6 %copy-start.10 = (f32[8]{0:T(128)S(1)}, f32[8]{0:T(128)}, u32[]{:S(2)}) copy-start(f32[8]{0:T(128)} %param.20) | copy-start | bytes 100
  7.8 34.0 %copy-start.6 = (s32[3456,1]{0,1:T(1,128)S(1)}, s32[3456,1]{0,1:T(1,128)}, u32[]{:S(2)}) copy-start(s32[3456,1]{0,1:T(1,128)} %param.17) | copy-start | bytes 41476
  7.8 34.0 %copy-start.9 = (s32[64]{0:T(128)S(1)}, s32[64]{0:T(128)}, u32[]{:S(2)}) copy-start(s32[64]{0:T(128)} %param.21) | copy-start | bytes 772
  7.9 30.5 %collective-permute-start = (bf16[6,3,96,384]{3,2,1,0:T(8,128)(2,1)S(1)}, bf16[6,3,96,384]{3,2,1,0:T(8,128)(2,1)}, u32[]{:S(2)}, u32[]{:S(2)}) collective-permute-start(bf16[6,3,96,384]{3,2,1,0:T(8,128)(2,1)S(1)} %get-tuple-element.128), channel_id=1, source_target_pairs={{0,1},{1,2},{2,3},{3,0},{4,5},{5,6},{6,7},{7,4},{8,9},{9,10},{10,1... | collective-permute-start | bytes 3981320 | tf_op jit(solution)/shard_map/ppermute | solution.py:17
  10.0 34.9 %collective-permute-start.1 = (bf16[6,3,96,384]{3,2,1,0:T(8,128)(2,1)S(1)}, bf16[6,3,96,384]{3,2,1,0:T(8,128)(2,1)}, u32[]{:S(2)}, u32[]{:S(2)}) collective-permute-start(bf16[6,3,96,384]{3,2,1,0:T(8,128)(2,1)S(1)} %get-tuple-element.128), channel_id=1, source_target_pairs={{0,3},{1,0},{2,1},{3,2},{4,7},{5,4},{6,5},{7,6},{8,11},{9,8},{10,9... | collective-permute-start | bytes 3981320 | tf_op jit(solution)/shard_map/ppermute | solution.py:20
  38.4 29.9 %collective-permute-start.2 = (bf16[6,3,96,384]{3,2,1,0:T(8,128)(2,1)}, bf16[6,3,96,384]{3,2,1,0:T(8,128)(2,1)}, u32[]{:S(2)}, u32[]{:S(2)}) collective-permute-start(bf16[6,3,96,384]{3,2,1,0:T(8,128)(2,1)} %collective-permute-done), channel_id=1, source_target_pairs={{0,1},{1,2},{2,3},{3,0},{4,5},{5,6},{6,7},{7,4},{8,9},{9,10},{10,1... | collective-permute-start | bytes 3981320 | tf_op jit(solution)/shard_map/ppermute | solution.py:17
  44.9 25.9 %copy-start.3 = (bf16[6,3,96,384]{3,2,1,0:T(8,128)(2,1)S(1)}, bf16[6,3,96,384]{3,2,1,0:T(8,128)(2,1)}, u32[]{:S(2)}) copy-start(bf16[6,3,96,384]{3,2,1,0:T(8,128)(2,1)} %param.13) | copy-start | bytes 3981316
  74.6 5.6 %collective-permute-start.3 = (bf16[6,3,10,384]{3,2,1,0:T(8,128)(2,1)S(1)}, bf16[6,3,10,384]{3,2,1,0:T(8,128)(2,1)S(1)}, u32[]{:S(2)}, u32[]{:S(2)}) collective-permute-start(bf16[6,3,10,384]{3,2,1,0:T(8,128)(2,1)S(1)} %get-tuple-element.125), channel_id=1, source_target_pairs={{0,1},{1,2},{2,3},{4,5},{5,6},{6,7},{8,9},{9,10},{10,11},{12,13},{... | collective-permute-start | bytes 414728 | tf_op jit(solution)/shard_map/ppermute | solution.py:34
  77.4 7.1 %collective-permute-start.4 = (bf16[6,3,10,384]{3,2,1,0:T(8,128)(2,1)S(1)}, bf16[6,3,10,384]{3,2,1,0:T(8,128)(2,1)}, u32[]{:S(2)}, u32[]{:S(2)}) collective-permute-start(bf16[6,3,10,384]{3,2,1,0:T(8,128)(2,1)S(1)} %get-tuple-element.126), channel_id=1, source_target_pairs={{1,0},{2,1},{3,2},{5,4},{6,5},{7,6},{9,8},{10,9},{11,10},{13,12},{... | collective-permute-start | bytes 414728 | tf_op jit(solution)/shard_map/ppermute | solution.py:35
  263.5 17.4 %copy-start.5 = (s32[3456]{0:T(1024)S(1)}, s32[3456]{0:T(1024)}, u32[]{:S(2)}) copy-start(s32[3456]{0:T(1024)} %param.18) | copy-start | bytes 41476
  263.5 89.6 %all-to-all-start = ((bf16[128,96,128]{2,1,0:T(8,128)(2,1)}), bf16[128,96,128]{2,1,0:T(8,128)(2,1)}, u32[]{:S(2)}, u32[]{:S(2)}) async-start(bf16[128,96,128]{2,1,0:T(8,128)(2,1)} %copy.71), calls=%async_computation | async-start | bytes 6291456 | tf_op jit(solution)/shard_map/all_to_all | solution.py:155
  360.8 79.7 %all-to-all-start.1 = ((bf16[128,96,128]{2,1,0:T(8,128)(2,1)}), bf16[128,96,128]{2,1,0:T(8,128)(2,1)}, u32[]{:S(2)}, u32[]{:S(2)}) async-start(bf16[128,96,128]{2,1,0:T(8,128)(2,1)} %copy.74), calls=%async_computation.1 | async-start | bytes 6291456 | tf_op jit(solution)/shard_map/all_to_all | solution.py:164
  440.5 3.3 copy-start.1
